TPU v7x, 32 devices: a whole 2x2x4 slice. The times are simulated.
32 devices in a mesh: sec: 4 (over y, x), tile: 8 (over z, core).
Axes of the slice: x: 2, y: 2, z: 4, core: 2. Of those that a mesh axis runs over, the one named last changes fastest.
Arguments:
- displacement: float32 [2, 16, 256, 256], P(None, 'sec', 'tile'), may hold values from -3 to 3
- coupling: float32 [4, 16, 256, 256], P(None, 'sec', 'tile'), may hold values from 0.1 to 1
- matches: float32 [4, 2, 16, 256, 256], P(None, None, 'sec', 'tile'), may hold values from -3 to 3
- step_sizes: float32 [2, 8], replicated, may hold values from 0.1 to 0.35
- restarts: int32 [2, 8], replicated, may hold values 0 or 1
- images: float32 [4, 64, 256, 256], P('sec', 'tile'), may hold values from 0 to 1
- block_anchor: int32 [4, 64], P('sec', 'tile'), may hold values from 0 to 32767
- block_dest: int32 [4, 64, 1], P('sec', 'tile'), may hold values from 0 to 7; in each aligned block of 8 rows (0 to 7, 8 to 15, ..., all dimensions but the last counted through in order) at most 2 rows name the same one
- block_slot: int32 [4, 64], P('sec', 'tile'), may hold values from 0 to 1
- block_offset: int32 [4, 64, 2], P('sec', 'tile'), may hold values from 0 to 128
- block_count: int32 [4, 8], P('sec', 'tile'), may hold values from 6 to 8, as said below
Outputs:
- aligned: float32 [2, 16, 256, 256], P(None, 'sec', 'tile')
- spans: float32 [64, 384, 384], P(('sec', 'tile'))
Inputs may be any that keep to these rules, and one draw needn't show every extreme that they name: `block_dest`: no tile index is named by more than 2 of the block slots of one device, and 2 is reached. `block_count`: some device uses all 8 slots.
All inputs are finite; a program needn't handle non-finite values.
Results may differ from a plain program's by a relative error of at most 0.0003.
Values sent between devices are 32-bit elements; how exact they have to be, the bound alone decides.
A program may use at most 128 MiB of HBM per device.

v0:
```python
import jax
import jax.numpy as jnp
from jax import lax
from jax.sharding import PartitionSpec as P

OUTER = 2
FIRE_STEPS = 8
BPP = 256
CH = 384
SPAN_DEV = 2
STIFFNESS = 1.0
MIXING = 0.1
EPSILON = 1e-06
SPEED_CAP = 0.1
PRECISE = lax.Precision.HIGHEST


def with_halo(array, sides, width):
    for axis, dim in sides:
        size, length = (lax.axis_size(axis), array.shape[dim])
        up = [(i, (i + 1) % size) for i in range(size - 1)]
        down = [(j, i) for i, j in up]
        last = lax.slice_in_dim(array, length - width, length, axis=dim)
        leading = lax.slice_in_dim(array, 0, width, axis=dim)
        before = lax.ppermute(last, axis, up)
        after = lax.ppermute(leading, axis, down)
        array = jnp.concatenate([before, array, after], axis=dim)
    return array


def forces(current, refer, coupling, matches, first_sec, sections_all):
    strain = current - refer
    rimmed = with_halo(strain, (("tile", 2),), 1)
    sides = jnp.pad(strain, ((0, 0), (0, 0), (0, 0), (1, 1)))
    summed = STIFFNESS * (
        rimmed[:, :, 2:] + rimmed[:, :, :-2] + sides[..., 2:] + sides[..., :-2] - 4.0 * strain
    )
    stacked = with_halo(current, (("sec", 1),), 2)
    sections_dev = current.shape[1]
    section = first_sec + jnp.arange(sections_dev)
    for which_k, reach in enumerate((-2, -1, 1, 2)):
        beside = stacked[:, 2 + reach : 2 + reach + sections_dev]
        usable = ((section + reach >= 0) & (section + reach < sections_all)).astype(jnp.float32)
        summed = summed + usable[None, :, None, None] * coupling[which_k][None] * (
            beside + matches[which_k] - current
        )
    return summed


def hat_rows(shift, size, source):
    row_pos = jnp.arange(size).astype(jnp.float32)[None, :, None]
    src_pos = jnp.arange(source).astype(jnp.float32)[None, None, :]
    return jnp.maximum(0.0, 1.0 - jnp.abs(row_pos - src_pos - shift[:, None, None]))


def warp_blocks(blocks_in, shift_y, shift_x):
    row_hats = hat_rows(shift_y, CH, BPP)
    col_hats = hat_rows(shift_x, CH, BPP)
    halfway = jnp.einsum("bij,bkj->bik", blocks_in, col_hats, precision=PRECISE)
    return jnp.einsum("bri,bik->brk", row_hats, halfway, precision=PRECISE)


def body(
    displacement,
    coupling,
    matches,
    step_sizes,
    restarts,
    images,
    block_anchor,
    block_dest,
    block_slot,
    block_offset,
    block_count,
):
    sections_dev = displacement.shape[1]
    first_sec = lax.axis_index("sec") * sections_dev
    sections_all = sections_dev * lax.axis_size("sec")
    node_total = 2.0 * sections_all * displacement.shape[3] * displacement.shape[3]
    current = displacement
    refer = displacement
    velocity = jnp.zeros_like(displacement)
    for outer_step in range(OUTER):
        for inner_step in range(FIRE_STEPS):
            delta = step_sizes[outer_step, inner_step]
            push = forces(current, refer, coupling, matches, first_sec, sections_all)
            velocity = velocity + delta * push
            speed_sq, push_sq = lax.psum(
                (jnp.sum(velocity * velocity), jnp.sum(push * push)), ("sec", "tile")
            )
            ratio = jnp.sqrt(speed_sq + EPSILON) / jnp.sqrt(push_sq + EPSILON)
            limit = jnp.minimum(1.0, SPEED_CAP / jnp.sqrt(speed_sq / node_total + EPSILON))
            retain = 1.0 - restarts[outer_step, inner_step].astype(jnp.float32)
            velocity = limit * retain * ((1.0 - MIXING) * velocity + MIXING * ratio * push)
            current = current + delta * velocity
        refer = current
        velocity = jnp.zeros_like(current)
    flat_disp = current.reshape(2, -1)
    moved = jnp.take(flat_disp, block_anchor[0], axis=1)
    blocks_here = block_anchor.shape[1]
    usable = (jnp.arange(blocks_here) < block_count[0, 0]).astype(jnp.float32)
    offsets = block_offset[0].astype(jnp.float32)
    shift_y = offsets[:, 0] + moved[0]
    shift_x = offsets[:, 1] + moved[1]
    owners = block_dest[0, :, 0]
    slot_hot = (block_slot[0][:, None] == jnp.arange(SPAN_DEV)[None, :]).astype(
        jnp.float32
    ) * usable[:, None]
    tiles = lax.axis_size("tile")
    capacity = max(2, 2 * blocks_here // tiles)
    owner_hot = (owners[:, None] == jnp.arange(tiles)[None, :]).astype(jnp.int32)
    rank_all = jnp.cumsum(owner_hot, axis=0) - owner_hot
    rank_own = jnp.sum(rank_all * owner_hot, axis=1)
    position = owners * capacity + rank_own
    placer = (position[None, :] == jnp.arange(tiles * capacity)[:, None]).astype(jnp.float32)
    send_blocks = jnp.einsum("sb,bij->sij", placer, images[0], precision=PRECISE).reshape(
        tiles, capacity, BPP, BPP
    )
    shifts_both = jnp.stack([shift_y, shift_x], axis=1)
    send_shift = jnp.dot(placer, shifts_both, precision=PRECISE).reshape(tiles, capacity, 2)
    send_select = jnp.dot(placer, slot_hot, precision=PRECISE).reshape(tiles, capacity, SPAN_DEV)
    blocks_in = lax.all_to_all(send_blocks, "tile", split_axis=0, concat_axis=0, tiled=True)
    shift_in = lax.all_to_all(send_shift, "tile", split_axis=0, concat_axis=0, tiled=True)
    select_in = lax.all_to_all(send_select, "tile", split_axis=0, concat_axis=0, tiled=True)
    sources = blocks_in.shape[0]
    items = blocks_in.shape[1]
    drawn = warp_blocks(
        blocks_in.reshape(sources * items, BPP, BPP),
        shift_in[..., 0].reshape(-1),
        shift_in[..., 1].reshape(-1),
    )
    drawn = drawn.reshape(sources, items, CH, CH)
    pieces = jnp.einsum("skc,skrq->kcrq", select_in, drawn, precision=PRECISE)
    spans = jnp.sum(pieces, axis=0)
    return (current, spans)


def solution(mesh):
    placed = (
        P(None, "sec", "tile", None),
        P(None, "sec", "tile", None),
        P(None, None, "sec", "tile", None),
        P(),
        P(),
        P("sec", "tile", None, None),
        P("sec", "tile"),
        P("sec", "tile", None),
        P("sec", "tile"),
        P("sec", "tile", None),
        P("sec", "tile"),
    )
    return jax.shard_map(
        body,
        mesh=mesh,
        in_specs=placed,
        out_specs=(P(None, "sec", "tile", None), P(("sec", "tile"), None, None)),
        check_vma=False,
    )
```

profile of v0, /device:TPU:0, one launch (start us, length us, event | category | flops | bytes accessed | tf_op | source)
XLA Modules:
  0.0 1109.9 jit_solution(523799049433969451)
XLA Ops:
  1.8 4.9 collective-permute-start.2
  23.0 43.6 %all-reduce.31 = (f32[]{:T(128)}, f32[]{:T(128)}) all-reduce(f32[]{:T(128)} %get-tuple-element.41, f32[]{:T(128)} %get-tuple-element.40), channel_id=1, replica_groups=mesh['sec'=4,'tile'=8] {'sec','tile'}, use_global_device_ids=true, to_apply=%region_1.2 | all-reduce | flops 2 | bytes 16 | tf_op jit(solution)/shard_map/psum | solution.py:88
  69.4 4.2 collective-permute-start.6
  83.4 42.6 %all-reduce.30 = (f32[]{:T(128)}, f32[]{:T(128)}) all-reduce(f32[]{:T(128)} %get-tuple-element.39, f32[]{:T(128)} %get-tuple-element.38), channel_id=1, replica_groups=mesh['sec'=4,'tile'=8] {'sec','tile'}, use_global_device_ids=true, to_apply=%region_5.6 | all-reduce | flops 2 | bytes 16 | tf_op jit(solution)/shard_map/psum | solution.py:88
  142.7 41.5 %all-reduce.29 = (f32[]{:T(128)}, f32[]{:T(128)}) all-reduce(f32[]{:T(128)} %get-tuple-element.37, f32[]{:T(128)} %get-tuple-element.36), channel_id=1, replica_groups=mesh['sec'=4,'tile'=8] {'sec','tile'}, use_global_device_ids=true, to_apply=%region_9.10 | all-reduce | flops 2 | bytes 16 | tf_op jit(solution)/shard_map/psum | solution.py:88
  200.4 42.6 %all-reduce.28 = (f32[]{:T(128)}, f32[]{:T(128)}) all-reduce(f32[]{:T(128)} %get-tuple-element.35, f32[]{:T(128)} %get-tuple-element.34), channel_id=1, replica_groups=mesh['sec'=4,'tile'=8] {'sec','tile'}, use_global_device_ids=true, to_apply=%region_13.14 | all-reduce | flops 2 | bytes 16 | tf_op jit(solution)/shard_map/psum | solution.py:88
  245.7 4.2 collective-permute-start.18
  259.0 41.5 %all-reduce.27 = (f32[]{:T(128)}, f32[]{:T(128)}) all-reduce(f32[]{:T(128)} %get-tuple-element.33, f32[]{:T(128)} %get-tuple-element.32), channel_id=1, replica_groups=mesh['sec'=4,'tile'=8] {'sec','tile'}, use_global_device_ids=true, to_apply=%region_17.18 | all-reduce | flops 2 | bytes 16 | tf_op jit(solution)/shard_map/psum | solution.py:88
  316.8 42.6 %all-reduce.26 = (f32[]{:T(128)}, f32[]{:T(128)}) all-reduce(f32[]{:T(128)} %get-tuple-element.31, f32[]{:T(128)} %get-tuple-element.30), channel_id=1, replica_groups=mesh['sec'=4,'tile'=8] {'sec','tile'}, use_global_device_ids=true, to_apply=%region_21.22 | all-reduce | flops 2 | bytes 16 | tf_op jit(solution)/shard_map/psum | solution.py:88
  375.4 41.5 %all-reduce.25 = (f32[]{:T(128)}, f32[]{:T(128)}) all-reduce(f32[]{:T(128)} %get-tuple-element.29, f32[]{:T(128)} %get-tuple-element.28), channel_id=1, replica_groups=mesh['sec'=4,'tile'=8] {'sec','tile'}, use_global_device_ids=true, to_apply=%region_25.26 | all-reduce | flops 2 | bytes 16 | tf_op jit(solution)/shard_map/psum | solution.py:88
  433.0 42.6 %all-reduce.24 = (f32[]{:T(128)}, f32[]{:T(128)}) all-reduce(f32[]{:T(128)} %get-tuple-element.27, f32[]{:T(128)} %get-tuple-element.26), channel_id=1, replica_groups=mesh['sec'=4,'tile'=8] {'sec','tile'}, use_global_device_ids=true, to_apply=%region_29.30 | all-reduce | flops 2 | bytes 16 | tf_op jit(solution)/shard_map/psum | solution.py:88
  478.4 4.2 collective-permute-start.34
  491.6 41.4 %all-reduce.23 = (f32[]{:T(128)}, f32[]{:T(128)}) all-reduce(f32[]{:T(128)} %get-tuple-element.25, f32[]{:T(128)} %get-tuple-element.24), channel_id=1, replica_groups=mesh['sec'=4,'tile'=8] {'sec','tile'}, use_global_device_ids=true, to_apply=%region_33.34 | all-reduce | flops 2 | bytes 16 | tf_op jit(solution)/shard_map/psum | solution.py:88
  535.7 4.2 collective-permute-start.38
  549.6 42.6 %all-reduce.22 = (f32[]{:T(128)}, f32[]{:T(128)}) all-reduce(f32[]{:T(128)} %get-tuple-element.23, f32[]{:T(128)} %get-tuple-element.22), channel_id=1, replica_groups=mesh['sec'=4,'tile'=8] {'sec','tile'}, use_global_device_ids=true, to_apply=%region_37.38 | all-reduce | flops 2 | bytes 16 | tf_op jit(solution)/shard_map/psum | solution.py:88
  612.3 42.3 %all-reduce.21 = (f32[]{:T(128)}, f32[]{:T(128)}) all-reduce(f32[]{:T(128)} %get-tuple-element.21, f32[]{:T(128)} %get-tuple-element.20), channel_id=1, replica_groups=mesh['sec'=4,'tile'=8] {'sec','tile'}, use_global_device_ids=true, to_apply=%region_41.42 | all-reduce | flops 2 | bytes 16 | tf_op jit(solution)/shard_map/psum | solution.py:88
  657.4 4.2 collective-permute-start.46
  670.8 42.6 %all-reduce.20 = (f32[]{:T(128)}, f32[]{:T(128)}) all-reduce(f32[]{:T(128)} %get-tuple-element.19, f32[]{:T(128)} %get-tuple-element.18), channel_id=1, replica_groups=mesh['sec'=4,'tile'=8] {'sec','tile'}, use_global_device_ids=true, to_apply=%region_45.46 | all-reduce | flops 2 | bytes 16 | tf_op jit(solution)/shard_map/psum | solution.py:88
  729.3 41.5 %all-reduce.19 = (f32[]{:T(128)}, f32[]{:T(128)}) all-reduce(f32[]{:T(128)} %get-tuple-element.17, f32[]{:T(128)} %get-tuple-element.16), channel_id=1, replica_groups=mesh['sec'=4,'tile'=8] {'sec','tile'}, use_global_device_ids=true, to_apply=%region_49.50 | all-reduce | flops 2 | bytes 16 | tf_op jit(solution)/shard_map/psum | solution.py:88
  773.7 4.2 collective-permute-start.54
  787.0 42.6 %all-reduce.18 = (f32[]{:T(128)}, f32[]{:T(128)}) all-reduce(f32[]{:T(128)} %get-tuple-element.15, f32[]{:T(128)} %get-tuple-element.14), channel_id=1, replica_groups=mesh['sec'=4,'tile'=8] {'sec','tile'}, use_global_device_ids=true, to_apply=%region_53.54 | all-reduce | flops 2 | bytes 16 | tf_op jit(solution)/shard_map/psum | solution.py:88
  845.6 41.7 %all-reduce.17 = (f32[]{:T(128)}, f32[]{:T(128)}) all-reduce(f32[]{:T(128)} %get-tuple-element.13, f32[]{:T(128)} %get-tuple-element.12), channel_id=1, replica_groups=mesh['sec'=4,'tile'=8] {'sec','tile'}, use_global_device_ids=true, to_apply=%region_57.58 | all-reduce | flops 2 | bytes 16 | tf_op jit(solution)/shard_map/psum | solution.py:88
  890.0 4.2 collective-permute-start.62
  903.2 42.6 %all-reduce.16 = (f32[]{:T(128)}, f32[]{:T(128)}) all-reduce(f32[]{:T(128)} %get-tuple-element.11, f32[]{:T(128)} %get-tuple-element.10), channel_id=1, replica_groups=mesh['sec'=4,'tile'=8] {'sec','tile'}, use_global_device_ids=true, to_apply=%region_61.62 | all-reduce | flops 2 | bytes 16 | tf_op jit(solution)/shard_map/psum | solution.py:88
  948.4 8.5 copy.33
  957.0 6.3 gather_fusion
  967.9 4.3 fusion.20
  975.5 5.1 all-to-all-start.2
  981.0 93.7 %all-to-all-done.2 = f32[8,2,256,256]{3,2,1,0:T(8,128)} async-done(((f32[8,2,256,256]{3,2,1,0:T(8,128)}), f32[8,2,256,256]{3,2,1,0:T(8,128)}, u32[]{:S(2)}, u32[]{:S(2)}) %all-to-all-start.2) | async-done | bytes 4194336 | tf_op jit(solution)/shard_map/all_to_all | solution.py:122
  1074.7 10.7 fusion.2
  1085.4 12.1 %fusion.7 = f32[16,384,384]{2,1,0:T(8,128)S(1)} fusion(f32[16,256,384]{2,1,0:T(8,128)S(1)} %fusion.2, f32[16]{0:T(128)S(1)} %sub.587, f32[384,256]{1,0:T(8,128)S(1)} %broadcast_subtract_fusion), kind=kOutput, calls=%fused_computation.8 | convolution fusion | flops 7254048768 | bytes 16121920 | tf_op jit(solution)/shard_map/bri,bik->brk/dot_general | solution.py:60
  1097.5 11.1 fusion.23
  (236 shorter events, 203.0 us)
Async XLA Ops:
  1.8 12.1 %collective-permute-start.2 = (f32[2,2,32,256]{3,2,1,0:T(8,128)S(1)}, f32[2,2,32,256]{3,2,1,0:T(8,128)S(1)}, u32[]{:S(2)}, u32[]{:S(2)}) collective-permute-start(f32[2,2,32,256]{3,2,1,0:T(8,128)S(1)} %get-tuple-element.205), channel_id=1, source_target_pairs={{0,8},{8,16},{16,24},{1,9},{9,17},{17,25},{2,10},{10,18},{18,26},{... | collective-permute-start | bytes 393224 | tf_op jit(solution)/shard_map/ppermute | solution.py:25
  6.6 12.6 %collective-permute-start.3 = (f32[2,2,32,256]{3,2,1,0:T(8,128)S(1)}, f32[2,2,32,256]{3,2,1,0:T(8,128)S(1)}, u32[]{:S(2)}, u32[]{:S(2)}) collective-permute-start(f32[2,2,32,256]{3,2,1,0:T(8,128)S(1)} %get-tuple-element.206), channel_id=1, source_target_pairs={{8,0},{16,8},{24,16},{9,1},{17,9},{25,17},{10,2},{18,10},{26,18},{... | collective-permute-start | bytes 393224 | tf_op jit(solution)/shard_map/ppermute | solution.py:26
  69.4 10.7 collective-permute-start.6
  73.6 7.4 collective-permute-start.7
  129.3 10.7 collective-permute-start.10
  187.1 10.7 collective-permute-start.14
  191.3 7.5 collective-permute-start.15
  245.7 10.7 collective-permute-start.18
  303.4 10.7 collective-permute-start.22
  307.6 7.5 collective-permute-start.23
  362.2 10.7 collective-permute-start.26
  366.4 7.5 collective-permute-start.27
  419.6 10.8 collective-permute-start.30
  423.8 7.4 collective-permute-start.31
  478.4 11.2 %collective-permute-start.34 = (f32[2,2,32,256]{3,2,1,0:T(8,128)S(1)}, f32[2,2,32,256]{3,2,1,0:T(8,128)S(1)}, u32[]{:S(2)}, u32[]{:S(2)}) collective-permute-start(f32[2,2,32,256]{3,2,1,0:T(8,128)S(1)} %get-tuple-element.172), channel_id=1, source_target_pairs={{0,8},{8,16},{16,24},{1,9},{9,17},{17,25},{2,10},{10,18},{18,26},{... | collective-permute-start | bytes 393224 | tf_op jit(solution)/shard_map/ppermute | solution.py:25
  482.6 7.4 collective-permute-start.35
  535.7 10.7 collective-permute-start.38
  595.8 14.8 %collective-permute-start.42 = (f32[2,2,32,256]{3,2,1,0:T(8,128)S(1)}, f32[2,2,32,256]{3,2,1,0:T(8,128)S(1)}, u32[]{:S(2)}, u32[]{:S(2)}) collective-permute-start(f32[2,2,32,256]{3,2,1,0:T(8,128)S(1)} %get-tuple-element.164), channel_id=1, source_target_pairs={{0,8},{8,16},{16,24},{1,9},{9,17},{17,25},{2,10},{10,18},{18,26},{... | collective-permute-start | bytes 393224 | tf_op jit(solution)/shard_map/ppermute | solution.py:25
  600.0 10.6 collective-permute-start.43
  601.3 9.3 collective-permute-start.40
  602.6 8.0 collective-permute-start.41
  606.5 357.9 %all-to-all-start = ((f32[8,2,2]{2,1,0:T(2,128)}), f32[8,2,2]{2,1,0:T(2,128)S(1)}, u32[]{:S(2)}, u32[]{:S(2)}) async-start(f32[8,2,2]{2,1,0:T(2,128)} %bitcast.43), calls=%async_computation | async-start | bytes 16384 | tf_op jit(solution)/shard_map/all_to_all | solution.py:124
  657.4 10.7 collective-permute-start.46
  661.6 7.4 collective-permute-start.47
  716.0 10.7 collective-permute-start.50
  773.7 10.7 collective-permute-start.54
  777.9 7.4 collective-permute-start.55
  832.4 10.7 collective-permute-start.58
  836.6 7.4 collective-permute-start.59
  890.0 10.7 collective-permute-start.62
  964.4 11.1 %all-to-all-start.1 = ((f32[8,2,2]{1,2,0:T(2,128)}), f32[8,2,2]{1,2,0:T(2,128)S(1)}, u32[]{:S(2)}, u32[]{:S(2)}) async-start(f32[8,2,2]{1,2,0:T(2,128)} %copy.34), calls=%async_computation.1 | async-start | bytes 16384 | tf_op jit(solution)/shard_map/all_to_all | solution.py:123
  975.5 99.2 %all-to-all-start.2 = ((f32[8,2,256,256]{3,2,1,0:T(8,128)}), f32[8,2,256,256]{3,2,1,0:T(8,128)}, u32[]{:S(2)}, u32[]{:S(2)}) async-start(f32[8,2,256,256]{3,2,1,0:T(8,128)} %copy.36), calls=%async_computation.2 | async-start | bytes 8388608 | tf_op jit(solution)/shard_map/all_to_all | solution.py:122
  (42 other events, 934.3 us)
where the time goes:
time: 1120 us; the launch traced here: 1110 us
  blocking collectives  676 us (60%)
  starting transfers between devices  170 us (15%)
  waiting for transfers between devices  109 us (10%)
  other arithmetic  45.2 us (4%)
  between operations  44.9 us (4%)
  matrix products  39.1 us (3%)
  local copies, waits for them, and re-layouts  26 us (2%)
    psum x16, blocking collectives, body(): lax.psum((jnp.sum(velocity * velocity), jnp.sum(push * push)), ('sec', 't...  676 us
    ppermute x32, starting transfers between devices, with_halo(): before = lax.ppermute(last, axis, up)  116 us
    all_to_all x1, waiting for transfers between devices, body(): lax.all_to_all(send_blocks, 'tile', split_axis=0, concat_axis=0, tiled=True)  93.7 us
    ppermute x32, starting transfers between devices, with_halo(): after = lax.ppermute(leading, axis, down)  41.3 us
    reduce_sum x16, other arithmetic, body(): jnp.sum(push * push)  29.4 us
  transfers between devices with their start and end apart: 67, of which 27 were waited for; matrix products, arithmetic and copies ran while one was open for 4% of the time, Pallas kernels for 0%

commit v1 on v0

--- a/solution.py
+++ b/solution.py
@@ -13,6 +13,24 @@
 EPSILON = 1e-06
 SPEED_CAP = 0.1
 PRECISE = lax.Precision.HIGHEST
+
+
+def copies_fix(v0, ndim_at, d0):
+    f_next, u1 = (jax.lax.axis_size("tile"), jax.lax.axis_index("tile"))
+    t_next = v0.shape[ndim_at] // f_next
+    a_next = list(v0.shape)
+    a_next[ndim_at] = t_next
+    inter = a_next[d0]
+    a_next[d0] = inter * f_next
+    current_block = jnp.zeros(a_next, v0.dtype)
+    for kk in [*range(f_next)]:
+        y2 = lax.dynamic_slice_in_dim(v0, (u1 ^ kk) * t_next, t_next, axis=ndim_at)
+        if kk:
+            y2 = jax.lax.ppermute(y2, "tile", [(m, m ^ kk) for m in range(f_next)])
+        current_block = lax.dynamic_update_slice_in_dim(
+            current_block, y2, (u1 ^ kk) * inter, axis=d0
+        )
+    return current_block
 
 
 def with_halo(array, sides, width):
@@ -119,7 +137,7 @@
     shifts_both = jnp.stack([shift_y, shift_x], axis=1)
     send_shift = jnp.dot(placer, shifts_both, precision=PRECISE).reshape(tiles, capacity, 2)
     send_select = jnp.dot(placer, slot_hot, precision=PRECISE).reshape(tiles, capacity, SPAN_DEV)
-    blocks_in = lax.all_to_all(send_blocks, "tile", split_axis=0, concat_axis=0, tiled=True)
+    blocks_in = copies_fix(send_blocks, 0, 0)
     shift_in = lax.all_to_all(send_shift, "tile", split_axis=0, concat_axis=0, tiled=True)
     select_in = lax.all_to_all(send_select, "tile", split_axis=0, concat_axis=0, tiled=True)
     sources = blocks_in.shape[0]

time: 1120 us -> 1070 us (0.955)
  waiting for transfers between devices: 109 us -> 9.52 us
  local copies, waits for them, and re-layouts: 26 us -> 43.2 us
  blocking collectives: 676 us -> 691 us
    all_to_all x1 -> x0, waiting for transfers between devices: 93.7 us -> none  [body(): lax.all_to_all(send_blocks, 'tile', split_axis=0, concat_axis=0, tiled=True)]
    psum x16, blocking collectives: 676 us -> 691 us  [body(): lax.psum((jnp.sum(velocity * velocity), jnp.sum(push * push)), ('sec', 't...]
    dynamic_update_slice x0 -> x8, local copies, waits for them, and re-layouts: none -> 14.1 us  [copies_fix(): lax.dynamic_update_slice_in_dim(current_block, y2, (u1 ^ kk) * inter, axi...]
  transfers between devices with their start and end apart: 67 -> 73, of which waited for: 27 -> 11; matrix products, arithmetic and copies ran while one was open for 4% -> 10% of each run, Pallas kernels for 0% -> 0%
where the time goes in v1:
time: 1070 us; the launch traced here: 1060 us
  blocking collectives  691 us (65%)
  starting transfers between devices  173 us (16%)
  other arithmetic  55.9 us (5%)
  between operations  45.6 us (4%)
  local copies, waits for them, and re-layouts  43.2 us (4%)
  matrix products  39.7 us (4%)
    psum x16, blocking collectives, body(): lax.psum((jnp.sum(velocity * velocity), jnp.sum(push * push)), ('sec', 't...  691 us
    ppermute x32, starting transfers between devices, with_halo(): before = lax.ppermute(last, axis, up)  117 us
    ppermute x32, starting transfers between devices, with_halo(): after = lax.ppermute(leading, axis, down)  41.3 us
    reduce_sum x16, other arithmetic, body(): jnp.sum(push * push)  32.4 us
  transfers between devices with their start and end apart: 73, of which 11 were waited for; matrix products, arithmetic and copies ran while one was open for 10% of the time, Pallas kernels for 0%

profile of v1, /device:TPU:0, one launch (start us, length us, event | category | flops | bytes accessed | tf_op | source)
XLA Modules:
  0.0 1058.6 jit_solution(11147196865366842248)
XLA Ops:
  1.6 4.9 collective-permute-start.2
  10.1 4.4 fusion.20
  29.0 44.2 %all-reduce.31 = (f32[]{:T(128)}, f32[]{:T(128)}) all-reduce(f32[]{:T(128)} %get-tuple-element.41, f32[]{:T(128)} %get-tuple-element.40), channel_id=1, replica_groups=mesh['sec'=4,'tile'=8] {'sec','tile'}, use_global_device_ids=true, to_apply=%region_1.2 | all-reduce | flops 2 | bytes 16 | tf_op jit(solution)/shard_map/psum | solution.py:106
  96.6 42.2 %all-reduce.30 = (f32[]{:T(128)}, f32[]{:T(128)}) all-reduce(f32[]{:T(128)} %get-tuple-element.39, f32[]{:T(128)} %get-tuple-element.38), channel_id=1, replica_groups=mesh['sec'=4,'tile'=8] {'sec','tile'}, use_global_device_ids=true, to_apply=%region_5.6 | all-reduce | flops 2 | bytes 16 | tf_op jit(solution)/shard_map/psum | solution.py:106
  143.1 4.2 collective-permute-start.10
  158.7 42.1 %all-reduce.29 = (f32[]{:T(128)}, f32[]{:T(128)}) all-reduce(f32[]{:T(128)} %get-tuple-element.37, f32[]{:T(128)} %get-tuple-element.36), channel_id=1, replica_groups=mesh['sec'=4,'tile'=8] {'sec','tile'}, use_global_device_ids=true, to_apply=%region_9.10 | all-reduce | flops 2 | bytes 16 | tf_op jit(solution)/shard_map/psum | solution.py:106
  203.8 4.2 collective-permute-start.14
  216.9 41.6 %all-reduce.28 = (f32[]{:T(128)}, f32[]{:T(128)}) all-reduce(f32[]{:T(128)} %get-tuple-element.35, f32[]{:T(128)} %get-tuple-element.34), channel_id=1, replica_groups=mesh['sec'=4,'tile'=8] {'sec','tile'}, use_global_device_ids=true, to_apply=%region_13.14 | all-reduce | flops 2 | bytes 16 | tf_op jit(solution)/shard_map/psum | solution.py:106
  261.5 4.2 collective-permute-start.18
  274.8 42.6 %all-reduce.27 = (f32[]{:T(128)}, f32[]{:T(128)}) all-reduce(f32[]{:T(128)} %get-tuple-element.33, f32[]{:T(128)} %get-tuple-element.32), channel_id=1, replica_groups=mesh['sec'=4,'tile'=8] {'sec','tile'}, use_global_device_ids=true, to_apply=%region_17.18 | all-reduce | flops 2 | bytes 16 | tf_op jit(solution)/shard_map/psum | solution.py:106
  320.2 4.2 collective-permute-start.22
  333.5 41.4 %all-reduce.26 = (f32[]{:T(128)}, f32[]{:T(128)}) all-reduce(f32[]{:T(128)} %get-tuple-element.31, f32[]{:T(128)} %get-tuple-element.30), channel_id=1, replica_groups=mesh['sec'=4,'tile'=8] {'sec','tile'}, use_global_device_ids=true, to_apply=%region_21.22 | all-reduce | flops 2 | bytes 16 | tf_op jit(solution)/shard_map/psum | solution.py:106
  390.8 42.7 %all-reduce.25 = (f32[]{:T(128)}, f32[]{:T(128)}) all-reduce(f32[]{:T(128)} %get-tuple-element.29, f32[]{:T(128)} %get-tuple-element.28), channel_id=1, replica_groups=mesh['sec'=4,'tile'=8] {'sec','tile'}, use_global_device_ids=true, to_apply=%region_25.26 | all-reduce | flops 2 | bytes 16 | tf_op jit(solution)/shard_map/psum | solution.py:106
  449.5 41.4 %all-reduce.24 = (f32[]{:T(128)}, f32[]{:T(128)}) all-reduce(f32[]{:T(128)} %get-tuple-element.27, f32[]{:T(128)} %get-tuple-element.26), channel_id=1, replica_groups=mesh['sec'=4,'tile'=8] {'sec','tile'}, use_global_device_ids=true, to_apply=%region_29.30 | all-reduce | flops 2 | bytes 16 | tf_op jit(solution)/shard_map/psum | solution.py:106
  506.7 42.8 %all-reduce.23 = (f32[]{:T(128)}, f32[]{:T(128)}) all-reduce(f32[]{:T(128)} %get-tuple-element.25, f32[]{:T(128)} %get-tuple-element.24), channel_id=1, replica_groups=mesh['sec'=4,'tile'=8] {'sec','tile'}, use_global_device_ids=true, to_apply=%region_33.34 | all-reduce | flops 2 | bytes 16 | tf_op jit(solution)/shard_map/psum | solution.py:106
  572.4 42.1 %all-reduce.22 = (f32[]{:T(128)}, f32[]{:T(128)}) all-reduce(f32[]{:T(128)} %get-tuple-element.23, f32[]{:T(128)} %get-tuple-element.22), channel_id=1, replica_groups=mesh['sec'=4,'tile'=8] {'sec','tile'}, use_global_device_ids=true, to_apply=%region_37.38 | all-reduce | flops 2 | bytes 16 | tf_op jit(solution)/shard_map/psum | solution.py:106
  618.0 4.2 collective-permute-start.42
  633.1 51.2 %all-reduce.21 = (f32[]{:T(128)}, f32[]{:T(128)}) all-reduce(f32[]{:T(128)} %get-tuple-element.21, f32[]{:T(128)} %get-tuple-element.20), channel_id=1, replica_groups=mesh['sec'=4,'tile'=8] {'sec','tile'}, use_global_device_ids=true, to_apply=%region_41.42 | all-reduce | flops 2 | bytes 16 | tf_op jit(solution)/shard_map/psum | solution.py:106
  704.0 44.3 %all-reduce.20 = (f32[]{:T(128)}, f32[]{:T(128)}) all-reduce(f32[]{:T(128)} %get-tuple-element.19, f32[]{:T(128)} %get-tuple-element.18), channel_id=1, replica_groups=mesh['sec'=4,'tile'=8] {'sec','tile'}, use_global_device_ids=true, to_apply=%region_45.46 | all-reduce | flops 2 | bytes 16 | tf_op jit(solution)/shard_map/psum | solution.py:106
  751.9 4.2 collective-permute-start.50
  768.2 43.7 %all-reduce.19 = (f32[]{:T(128)}, f32[]{:T(128)}) all-reduce(f32[]{:T(128)} %get-tuple-element.17, f32[]{:T(128)} %get-tuple-element.16), channel_id=1, replica_groups=mesh['sec'=4,'tile'=8] {'sec','tile'}, use_global_device_ids=true, to_apply=%region_49.50 | all-reduce | flops 2 | bytes 16 | tf_op jit(solution)/shard_map/psum | solution.py:106
  815.5 4.2 collective-permute-start.54
  831.1 43.0 %all-reduce.18 = (f32[]{:T(128)}, f32[]{:T(128)}) all-reduce(f32[]{:T(128)} %get-tuple-element.15, f32[]{:T(128)} %get-tuple-element.14), channel_id=1, replica_groups=mesh['sec'=4,'tile'=8] {'sec','tile'}, use_global_device_ids=true, to_apply=%region_53.54 | all-reduce | flops 2 | bytes 16 | tf_op jit(solution)/shard_map/psum | solution.py:106
  877.9 4.2 collective-permute-start.58
  892.6 44.6 %all-reduce.17 = (f32[]{:T(128)}, f32[]{:T(128)}) all-reduce(f32[]{:T(128)} %get-tuple-element.13, f32[]{:T(128)} %get-tuple-element.12), channel_id=1, replica_groups=mesh['sec'=4,'tile'=8] {'sec','tile'}, use_global_device_ids=true, to_apply=%region_57.58 | all-reduce | flops 2 | bytes 16 | tf_op jit(solution)/shard_map/psum | solution.py:106
  940.0 4.2 collective-permute-start.62
  953.4 41.4 %all-reduce.16 = (f32[]{:T(128)}, f32[]{:T(128)}) all-reduce(f32[]{:T(128)} %get-tuple-element.11, f32[]{:T(128)} %get-tuple-element.10), channel_id=1, replica_groups=mesh['sec'=4,'tile'=8] {'sec','tile'}, use_global_device_ids=true, to_apply=%region_61.62 | all-reduce | flops 2 | bytes 16 | tf_op jit(solution)/shard_map/psum | solution.py:106
  997.6 8.6 copy.47
  1006.2 6.4 gather_fusion
  1023.3 10.5 fusion.2
  1033.8 12.1 %fusion.7 = f32[16,384,384]{2,1,0:T(8,128)S(1)} fusion(f32[16,256,384]{2,1,0:T(8,128)S(1)} %fusion.2, f32[16]{0:T(128)S(1)} %sub.587, f32[384,256]{1,0:T(8,128)S(1)} %broadcast_subtract_fusion), kind=kOutput, calls=%fused_computation.8 | convolution fusion | flops 7254048768 | bytes 16121920 | tf_op jit(solution)/shard_map/bri,bik->brk/dot_general | solution.py:78
  1045.9 11.2 %fusion.23 = f32[2,384,384]{2,0,1:T(2,128)S(1)} fusion(f32[8,2,384,384]{3,2,1,0:T(8,128)S(1)} %bitcast.214, f32[8,2,2]{0,2,1:T(2,128)S(1)} %copy-done.6), kind=kOutput, calls=%fused_computation.24 | convolution fusion | flops 56623104 | bytes 10616960 | tf_op jit(solution)/shard_map/skc,skrq->kcrq/dot_general | solution.py:151
  (271 shorter events, 226.1 us)
Async XLA Ops:
  1.6 20.4 %collective-permute-start.2 = (f32[2,2,32,256]{3,2,1,0:T(8,128)S(1)}, f32[2,2,32,256]{3,2,1,0:T(8,128)S(1)}, u32[]{:S(2)}, u32[]{:S(2)}) collective-permute-start(f32[2,2,32,256]{3,2,1,0:T(8,128)S(1)} %get-tuple-element.213), channel_id=1, source_target_pairs={{0,8},{8,16},{16,24},{1,9},{9,17},{17,25},{2,10},{10,18},{18,26},{... | collective-permute-start | bytes 393224 | tf_op jit(solution)/shard_map/ppermute | solution.py:43
  6.5 20.0 %collective-permute-start.3 = (f32[2,2,32,256]{3,2,1,0:T(8,128)S(1)}, f32[2,2,32,256]{3,2,1,0:T(8,128)S(1)}, u32[]{:S(2)}, u32[]{:S(2)}) collective-permute-start(f32[2,2,32,256]{3,2,1,0:T(8,128)S(1)} %get-tuple-element.214), channel_id=1, source_target_pairs={{8,0},{16,8},{24,16},{9,1},{17,9},{25,17},{10,2},{18,10},{26,18},{... | collective-permute-start | bytes 393224 | tf_op jit(solution)/shard_map/ppermute | solution.py:44
  18.5 606.3 %collective-permute-start.64 = (f32[1,2,256,256]{3,0,2,1:T(1,128)}, f32[1,2,256,256]{3,0,2,1:T(1,128)}, u32[]{:S(2)}, u32[]{:S(2)}) collective-permute-start(f32[1,2,256,256]{3,0,2,1:T(1,128)} %get-tuple-element.142), channel_id=1, source_target_pairs={{0,1},{1,0},{2,3},{3,2},{4,5},{5,4},{6,7},{7,6},{8,9},{9,8},{10,11... | collective-permute-start | bytes 1572872 | tf_op jit(solution)/shard_map/ppermute | solution.py:29
  76.5 16.4 %collective-permute-start.6 = (f32[2,2,32,256]{3,2,1,0:T(8,128)}, f32[2,2,32,256]{3,2,1,0:T(8,128)S(1)}, u32[]{:S(2)}, u32[]{:S(2)}) collective-permute-start(f32[2,2,32,256]{3,2,1,0:T(8,128)} %get-tuple-element.208), channel_id=1, source_target_pairs={{0,8},{8,16},{16,24},{1,9},{9,17},{17,25},{2,10},{10,18},{18,26},{... | collective-permute-start | bytes 393224 | tf_op jit(solution)/shard_map/ppermute | solution.py:43
  80.7 12.3 %collective-permute-start.7 = (f32[2,2,32,256]{3,2,1,0:T(8,128)S(1)}, f32[2,2,32,256]{3,2,1,0:T(8,128)S(1)}, u32[]{:S(2)}, u32[]{:S(2)}) collective-permute-start(f32[2,2,32,256]{3,2,1,0:T(8,128)S(1)} %get-tuple-element.209), channel_id=1, source_target_pairs={{8,0},{16,8},{24,16},{9,1},{17,9},{25,17},{10,2},{18,10},{26,18},{... | collective-permute-start | bytes 393224 | tf_op jit(solution)/shard_map/ppermute | solution.py:44
  82.6 10.3 collective-permute-start.4
  89.0 479.8 %all-to-all-start = ((f32[8,2,2]{2,1,0:T(2,128)}), f32[8,2,2]{2,1,0:T(2,128)S(1)}, u32[]{:S(2)}, u32[]{:S(2)}) async-start(f32[8,2,2]{2,1,0:T(2,128)} %bitcast.217), calls=%async_computation | async-start | bytes 16384 | tf_op jit(solution)/shard_map/all_to_all | solution.py:142
  143.1 13.7 %collective-permute-start.10 = (f32[2,2,32,256]{3,2,1,0:T(8,128)S(1)}, f32[2,2,32,256]{3,2,1,0:T(8,128)S(1)}, u32[]{:S(2)}, u32[]{:S(2)}) collective-permute-start(f32[2,2,32,256]{3,2,1,0:T(8,128)S(1)} %get-tuple-element.204), channel_id=1, source_target_pairs={{0,8},{8,16},{16,24},{1,9},{9,17},{17,25},{2,10},{10,18},{18,26},{... | collective-permute-start | bytes 393224 | tf_op jit(solution)/shard_map/ppermute | solution.py:43
  147.3 9.6 collective-permute-start.11
  203.8 10.7 %collective-permute-start.14 = (f32[2,2,32,256]{3,2,1,0:T(8,128)S(1)}, f32[2,2,32,256]{3,2,1,0:T(8,128)S(1)}, u32[]{:S(2)}, u32[]{:S(2)}) collective-permute-start(f32[2,2,32,256]{3,2,1,0:T(8,128)S(1)} %get-tuple-element.200), channel_id=1, source_target_pairs={{0,8},{8,16},{16,24},{1,9},{9,17},{17,25},{2,10},{10,18},{18,26},{... | collective-permute-start | bytes 393224 | tf_op jit(solution)/shard_map/ppermute | solution.py:43
  261.5 10.7 %collective-permute-start.18 = (f32[2,2,32,256]{3,2,1,0:T(8,128)S(1)}, f32[2,2,32,256]{3,2,1,0:T(8,128)S(1)}, u32[]{:S(2)}, u32[]{:S(2)}) collective-permute-start(f32[2,2,32,256]{3,2,1,0:T(8,128)S(1)} %get-tuple-element.196), channel_id=1, source_target_pairs={{0,8},{8,16},{16,24},{1,9},{9,17},{17,25},{2,10},{10,18},{18,26},{... | collective-permute-start | bytes 393224 | tf_op jit(solution)/shard_map/ppermute | solution.py:43
  320.2 10.7 %collective-permute-start.22 = (f32[2,2,32,256]{3,2,1,0:T(8,128)S(1)}, f32[2,2,32,256]{3,2,1,0:T(8,128)S(1)}, u32[]{:S(2)}, u32[]{:S(2)}) collective-permute-start(f32[2,2,32,256]{3,2,1,0:T(8,128)S(1)} %get-tuple-element.192), channel_id=1, source_target_pairs={{0,8},{8,16},{16,24},{1,9},{9,17},{17,25},{2,10},{10,18},{18,26},{... | collective-permute-start | bytes 393224 | tf_op jit(solution)/shard_map/ppermute | solution.py:43
  377.7 11.0 %collective-permute-start.26 = (f32[2,2,32,256]{3,2,1,0:T(8,128)S(1)}, f32[2,2,32,256]{3,2,1,0:T(8,128)S(1)}, u32[]{:S(2)}, u32[]{:S(2)}) collective-permute-start(f32[2,2,32,256]{3,2,1,0:T(8,128)S(1)} %get-tuple-element.188), channel_id=1, source_target_pairs={{0,8},{8,16},{16,24},{1,9},{9,17},{17,25},{2,10},{10,18},{18,26},{... | collective-permute-start | bytes 393224 | tf_op jit(solution)/shard_map/ppermute | solution.py:43
  436.3 11.0 %collective-permute-start.30 = (f32[2,2,32,256]{3,2,1,0:T(8,128)S(1)}, f32[2,2,32,256]{3,2,1,0:T(8,128)S(1)}, u32[]{:S(2)}, u32[]{:S(2)}) collective-permute-start(f32[2,2,32,256]{3,2,1,0:T(8,128)S(1)} %get-tuple-element.184), channel_id=1, source_target_pairs={{0,8},{8,16},{16,24},{1,9},{9,17},{17,25},{2,10},{10,18},{18,26},{... | collective-permute-start | bytes 393224 | tf_op jit(solution)/shard_map/ppermute | solution.py:43
  493.6 11.1 %collective-permute-start.34 = (f32[2,2,32,256]{3,2,1,0:T(8,128)S(1)}, f32[2,2,32,256]{3,2,1,0:T(8,128)S(1)}, u32[]{:S(2)}, u32[]{:S(2)}) collective-permute-start(f32[2,2,32,256]{3,2,1,0:T(8,128)S(1)} %get-tuple-element.180), channel_id=1, source_target_pairs={{0,8},{8,16},{16,24},{1,9},{9,17},{17,25},{2,10},{10,18},{18,26},{... | collective-permute-start | bytes 393224 | tf_op jit(solution)/shard_map/ppermute | solution.py:43
  552.1 17.3 %collective-permute-start.38 = (f32[2,2,32,256]{3,2,1,0:T(8,128)S(1)}, f32[2,2,32,256]{3,2,1,0:T(8,128)S(1)}, u32[]{:S(2)}, u32[]{:S(2)}) collective-permute-start(f32[2,2,32,256]{3,2,1,0:T(8,128)S(1)} %get-tuple-element.176), channel_id=1, source_target_pairs={{0,8},{8,16},{16,24},{1,9},{9,17},{17,25},{2,10},{10,18},{18,26},{... | collective-permute-start | bytes 393224 | tf_op jit(solution)/shard_map/ppermute | solution.py:43
  556.3 13.1 %collective-permute-start.39 = (f32[2,2,32,256]{3,2,1,0:T(8,128)S(1)}, f32[2,2,32,256]{3,2,1,0:T(8,128)S(1)}, u32[]{:S(2)}, u32[]{:S(2)}) collective-permute-start(f32[2,2,32,256]{3,2,1,0:T(8,128)S(1)} %get-tuple-element.177), channel_id=1, source_target_pairs={{8,0},{16,8},{24,16},{9,1},{17,9},{25,17},{10,2},{18,10},{26,18},{... | collective-permute-start | bytes 393224 | tf_op jit(solution)/shard_map/ppermute | solution.py:44
  558.2 11.2 %collective-permute-start.36 = (f32[2,4,1,256]{3,2,1,0:T(1,128)}, f32[2,4,1,256]{3,2,1,0:T(1,128)S(1)}, u32[]{:S(2)}, u32[]{:S(2)}) collective-permute-start(f32[2,4,1,256]{3,2,1,0:T(1,128)} %get-tuple-element.174), channel_id=1, source_target_pairs={{1,0},{2,1},{3,2},{4,3},{5,4},{6,5},{7,6},{9,8},{10,9},{11,10},{12... | collective-permute-start | bytes 24584 | tf_op jit(solution)/shard_map/ppermute | solution.py:44
  559.5 9.9 collective-permute-start.37
  569.4 125.4 %collective-permute-start.65 = (f32[1,2,256,256]{3,0,2,1:T(1,128)}, f32[1,2,256,256]{3,0,2,1:T(1,128)}, u32[]{:S(2)}, u32[]{:S(2)}) collective-permute-start(f32[1,2,256,256]{3,0,2,1:T(1,128)} %get-tuple-element.141), channel_id=1, source_target_pairs={{0,2},{1,3},{2,0},{3,1},{4,6},{5,7},{6,4},{7,5},{8,10},{9,11},{10,... | collective-permute-start | bytes 1572872 | tf_op jit(solution)/shard_map/ppermute | solution.py:29
  618.0 12.7 %collective-permute-start.42 = (f32[2,2,32,256]{3,2,1,0:T(8,128)S(1)}, f32[2,2,32,256]{3,2,1,0:T(8,128)S(1)}, u32[]{:S(2)}, u32[]{:S(2)}) collective-permute-start(f32[2,2,32,256]{3,2,1,0:T(8,128)S(1)} %get-tuple-element.172), channel_id=1, source_target_pairs={{0,8},{8,16},{16,24},{1,9},{9,17},{17,25},{2,10},{10,18},{18,26},{... | collective-permute-start | bytes 393224 | tf_op jit(solution)/shard_map/ppermute | solution.py:43
  629.7 129.0 %collective-permute-start.66 = (f32[1,2,256,256]{3,0,2,1:T(1,128)}, f32[1,2,256,256]{3,0,2,1:T(1,128)}, u32[]{:S(2)}, u32[]{:S(2)}) collective-permute-start(f32[1,2,256,256]{3,0,2,1:T(1,128)} %get-tuple-element.140), channel_id=1, source_target_pairs={{0,3},{1,2},{2,1},{3,0},{4,7},{5,6},{6,5},{7,4},{8,11},{9,10},{10,... | collective-permute-start | bytes 1572872 | tf_op jit(solution)/shard_map/ppermute | solution.py:29
  688.0 13.6 %collective-permute-start.46 = (f32[2,2,32,256]{3,2,1,0:T(8,128)S(1)}, f32[2,2,32,256]{3,2,1,0:T(8,128)S(1)}, u32[]{:S(2)}, u32[]{:S(2)}) collective-permute-start(f32[2,2,32,256]{3,2,1,0:T(8,128)S(1)} %get-tuple-element.168), channel_id=1, source_target_pairs={{0,8},{8,16},{16,24},{1,9},{9,17},{17,25},{2,10},{10,18},{18,26},{... | collective-permute-start | bytes 393224 | tf_op jit(solution)/shard_map/ppermute | solution.py:43
  699.8 122.6 %collective-permute-start.67 = (f32[1,2,256,256]{3,0,2,1:T(1,128)}, f32[1,2,256,256]{3,0,2,1:T(1,128)}, u32[]{:S(2)}, u32[]{:S(2)}) collective-permute-start(f32[1,2,256,256]{3,0,2,1:T(1,128)} %get-tuple-element.139), channel_id=1, source_target_pairs={{0,4},{1,5},{2,6},{3,7},{4,0},{5,1},{6,2},{7,3},{8,12},{9,13},{10,... | collective-permute-start | bytes 1572872 | tf_op jit(solution)/shard_map/ppermute | solution.py:29
  751.9 13.9 %collective-permute-start.50 = (f32[2,2,32,256]{3,2,1,0:T(8,128)S(1)}, f32[2,2,32,256]{3,2,1,0:T(8,128)S(1)}, u32[]{:S(2)}, u32[]{:S(2)}) collective-permute-start(f32[2,2,32,256]{3,2,1,0:T(8,128)S(1)} %get-tuple-element.164), channel_id=1, source_target_pairs={{0,8},{8,16},{16,24},{1,9},{9,17},{17,25},{2,10},{10,18},{18,26},{... | collective-permute-start | bytes 393224 | tf_op jit(solution)/shard_map/ppermute | solution.py:43
  756.1 9.7 collective-permute-start.51
  763.7 121.0 %collective-permute-start.68 = (f32[1,2,256,256]{3,0,2,1:T(1,128)}, f32[1,2,256,256]{3,0,2,1:T(1,128)}, u32[]{:S(2)}, u32[]{:S(2)}) collective-permute-start(f32[1,2,256,256]{3,0,2,1:T(1,128)} %get-tuple-element.138), channel_id=1, source_target_pairs={{0,5},{1,4},{2,7},{3,6},{4,1},{5,0},{6,3},{7,2},{8,13},{9,12},{10,... | collective-permute-start | bytes 1572872 | tf_op jit(solution)/shard_map/ppermute | solution.py:29
  815.5 13.3 %collective-permute-start.54 = (f32[2,2,32,256]{3,2,1,0:T(8,128)S(1)}, f32[2,2,32,256]{3,2,1,0:T(8,128)S(1)}, u32[]{:S(2)}, u32[]{:S(2)}) collective-permute-start(f32[2,2,32,256]{3,2,1,0:T(8,128)S(1)} %get-tuple-element.160), channel_id=1, source_target_pairs={{0,8},{8,16},{16,24},{1,9},{9,17},{17,25},{2,10},{10,18},{18,26},{... | collective-permute-start | bytes 393224 | tf_op jit(solution)/shard_map/ppermute | solution.py:43
  827.3 119.5 %collective-permute-start.69 = (f32[1,2,256,256]{3,0,2,1:T(1,128)}, f32[1,2,256,256]{3,0,2,1:T(1,128)}, u32[]{:S(2)}, u32[]{:S(2)}) collective-permute-start(f32[1,2,256,256]{3,0,2,1:T(1,128)} %get-tuple-element.137), channel_id=1, source_target_pairs={{0,6},{1,7},{2,4},{3,5},{4,2},{5,3},{6,0},{7,1},{8,14},{9,15},{10,... | collective-permute-start | bytes 1572872 | tf_op jit(solution)/shard_map/ppermute | solution.py:29
  877.9 13.1 %collective-permute-start.58 = (f32[2,2,32,256]{3,2,1,0:T(8,128)S(1)}, f32[2,2,32,256]{3,2,1,0:T(8,128)S(1)}, u32[]{:S(2)}, u32[]{:S(2)}) collective-permute-start(f32[2,2,32,256]{3,2,1,0:T(8,128)S(1)} %get-tuple-element.156), channel_id=1, source_target_pairs={{0,8},{8,16},{16,24},{1,9},{9,17},{17,25},{2,10},{10,18},{18,26},{... | collective-permute-start | bytes 393224 | tf_op jit(solution)/shard_map/ppermute | solution.py:43
  889.7 127.8 %collective-permute-start.70 = (f32[1,2,256,256]{3,0,2,1:T(1,128)}, f32[1,2,256,256]{3,0,2,1:T(1,128)}, u32[]{:S(2)}, u32[]{:S(2)}) collective-permute-start(f32[1,2,256,256]{3,0,2,1:T(1,128)} %get-tuple-element.136), channel_id=1, source_target_pairs={{0,7},{1,6},{2,5},{3,4},{4,3},{5,2},{6,1},{7,0},{8,15},{9,14},{10,... | collective-permute-start | bytes 1572872 | tf_op jit(solution)/shard_map/ppermute | solution.py:29
  940.0 11.8 %collective-permute-start.62 = (f32[2,2,32,256]{3,2,1,0:T(8,128)S(1)}, f32[2,2,32,256]{3,2,1,0:T(8,128)S(1)}, u32[]{:S(2)}, u32[]{:S(2)}) collective-permute-start(f32[2,2,32,256]{3,2,1,0:T(8,128)S(1)} %get-tuple-element.152), channel_id=1, source_target_pairs={{0,8},{8,16},{16,24},{1,9},{9,17},{17,25},{2,10},{10,18},{18,26},{... | collective-permute-start | bytes 393224 | tf_op jit(solution)/shard_map/ppermute | solution.py:43
  (55 other events, 735.0 us)
